TPU v7x, 128 devices: a whole 4x4x4 slice. The times are simulated.
128 devices in a mesh: row: 8 (over x, y_hi), col: 16 (over y_lo, z, core).
Axes of the slice: x: 4, y: 4 (y_hi: 2, y_lo: 2; y = y_hi * 2 + y_lo), z: 4, core: 2. Of those that a mesh axis runs over, the one named last changes fastest.
Arguments:
- front_trailing: float32 [16384, 16384], P('row', 'col'), may hold values from -6 to 6
- panel_columns: float32 [16384, 1024], P('row', 'col'), may hold values from -0.1875 to 0.1875
- panel_rows: float32 [1024, 16384], P('row', 'col'), may hold values from -6 to 6
- pivots: int32 [1024], replicated, may hold values from 0 to 1023, each once
- diag_inverse: float32 [1024, 1024], replicated, may hold values from -0.1875 to 0.1875
- test_matrix: float32 [16384, 512], P('col'), may hold values from -0.046875 to 0.046875
Outputs:
- schur: float32 [16384, 16384], P('row', 'col')
- off_samples: float32 [16384, 512], P(('row', 'col'))
- leaf_blocks: float32 [16384, 128], P(('row', 'col'))
- group_gram: float32 [8, 512, 512], P('row')
Inputs may be any that keep to these rules, and one draw needn't show every extreme that they name: pivots names each of 0 to 1023 once.
All inputs are finite; a program needn't handle non-finite values.
Results may differ from a plain program's by a relative error of at most 0.000084.
Values sent between devices are 32-bit elements; how exact they have to be, the bound alone decides.
A program may use at most 128 MiB of HBM per device.

v0:
```python
import jax
import jax.numpy as jnp
from jax import lax
from jax.sharding import PartitionSpec as P

LEAF = 128


def product(left, right):
    return jnp.dot(left, right, precision=lax.Precision.HIGH, preferred_element_type=jnp.float32)


def body(front_trailing, panel_columns, panel_rows, pivots, diag_inverse, test_matrix):
    col_count = lax.axis_size("col")
    row_count = lax.axis_size("row")
    row_index = lax.axis_index("row")
    col_index = lax.axis_index("col")
    height, width = front_trailing.shape
    upper_full = lax.all_gather(panel_rows, "row", axis=0, tiled=True)
    left = lax.all_gather(panel_columns, "col", axis=1, tiled=True)
    upper = jnp.take(upper_full, pivots, axis=0)
    weight = product(diag_inverse, upper)
    schur = front_trailing - product(left, weight)
    rows = row_index * height + jnp.arange(height, dtype=jnp.int32)
    cols = col_index * width + jnp.arange(width, dtype=jnp.int32)
    same_leaf = rows[:, None] // LEAF == cols[None, :] // LEAF
    masked = jnp.where(same_leaf, jnp.zeros_like(schur), schur)
    partial = product(masked, test_matrix)
    count = width // LEAF
    ratio = col_count // row_count
    leaves = height // LEAF
    kept = []
    for leaf in range(leaves):
        held = col_index == row_index * ratio + leaf // count
        block = schur[
            leaf * LEAF : (leaf + 1) * LEAF, leaf % count * LEAF : (leaf % count + 1) * LEAF
        ]
        kept.append(jnp.where(held, block, jnp.zeros_like(block)))
    both = jnp.concatenate([partial, jnp.concatenate(kept, axis=0)], axis=1)
    own = lax.psum_scatter(both, "col", scatter_dimension=0, tiled=True)
    own_samples = own[:, : partial.shape[1]]
    leaf_blocks = own[:, partial.shape[1] :]
    gram = lax.dot_general(
        own_samples,
        own_samples,
        (((0,), (0,)), ((), ())),
        precision=lax.Precision.HIGH,
        preferred_element_type=jnp.float32,
    )
    gram = lax.psum(gram, "col")
    route = [(i, i ^ 1) for i in range(row_count)]
    gram = gram + lax.ppermute(gram, "row", route)
    group_gram = (gram / (2 * height))[None]
    return (schur, own_samples, leaf_blocks, group_gram)


def solution(mesh):
    placed = (P("row", "col"), P("row", "col"), P("row", "col"), P(), P(), P("col", None))
    return jax.shard_map(
        body,
        mesh=mesh,
        in_specs=placed,
        out_specs=(
            P("row", "col"),
            P(("row", "col"), None),
            P(("row", "col"), None),
            P("row", None, None),
        ),
        check_vma=False,
    )
```

profile of v0, /device:TPU:0, one launch (start us, length us, event | category | flops | bytes accessed | tf_op | source)
XLA Modules:
  0.0 392.7 jit_solution(6487991175751841340)
XLA Ops:
  7.2 0.0 all-gather.3.cloned.1.call-start
  7.2 0.7 all-gather.3.cloned.1.call-update
  7.9 0.0 all-gather.5.cloned.1.call-start
  8.0 0.7 all-gather.5.cloned.1.call-update
  8.7 0.0 reduce-scatter.2.cloned.1.call-start
  8.7 9.1 %copy.10 = f32[2048,1024]{0,1:T(8,128)} copy(f32[2048,1024]{1,0:T(8,128)} %param.6) | data formatting | bytes 16777216 | tf_op args[0]
  17.9 66.5 %all-gather.3.cloned.1.call-done = f32[1024,1024]{1,0:T(8,128)} async-done(((f32[128,1024]{1,0:T(8,128)}), f32[1024,1024]{1,0:T(8,128)}) %all-gather.3.cloned.1.call-update) | async-done | bytes 4194320 | tf_op jit(solution)/shard_map/all_gather | solution.py:19
  84.4 8.6 %gather_fusion = f32[1024,1024]{1,0:T(8,128)} fusion(f32[1024,1024]{1,0:T(8,128)} %all-gather.3.cloned.1.call-done, s32[1024]{0:T(1024)S(1)} %fusion.32), kind=kCustom, calls=%fused_computation | custom fusion | bytes 8392704 | tf_op jit(solution)/shard_map/jit(_take)/gather | solution.py:21
  93.0 17.9 %fusion.5 = f32[1024,1024]{1,0:T(8,128)} fusion(f32[1024,1024]{1,0:T(8,128)} %param.10, f32[1024,1024]{1,0:T(8,128)} %gather_fusion, pred[1024]{0:T(1024)(128)(4,1)S(1)} %compare_and_fusion), kind=kOutput, calls=%fused_computation.8 | convolution fusion | flops 6443499520 | bytes 12583936 | tf_op jit(solution)/shard_map/dot_general | solution.py:10
  110.9 25.2 %all-gather.5.cloned.1.call-done = f32[2048,1024]{0,1:T(8,128)} async-done(((f32[2048,64]{0,1:T(8,128)}), f32[2048,1024]{0,1:T(8,128)}) %all-gather.5.cloned.1.call-update) | async-done | bytes 8388624 | tf_op jit(solution)/shard_map/all_gather | solution.py:20
  136.1 17.8 %bitcast_subtract_fusion = f32[2048,1024]{0,1:T(8,128)S(1)} fusion(f32[2048,1024]{0,1:T(8,128)} %copy.10, f32[1024,1024]{1,0:T(8,128)} %fusion.5, f32[2048,1024]{0,1:T(8,128)} %all-gather.5.cloned.1.call-done), kind=kOutput, calls=%fused_computation.1 | convolution fusion | flops 12886999040 | bytes 29360128 | tf_op jit(solution)/shard_map/dot_general | solution.py:10
  154.3 7.6 %fusion = f32[2048,512]{0,1:T(8,128)S(1)} fusion(f32[1024,512]{1,0:T(8,128)S(1)} %copy-done, f32[2048,1024]{0,1:T(8,128)S(1)} %bitcast_subtract_fusion, s32[2048]{0:T(1024)S(1)} %add_select_fusion, s32[1024]{0:T(1024)S(1)} %add_select_fusion.1), kind=kOutput, calls=%fused_computation.2 | convolution fusion | flops 6446645248 | bytes 14692352 | tf_op jit(solution)/shard_map/dot_general | solution.py:10
  161.9 3.0 pad_maximum_fusion
  164.9 0.0 reduce-scatter.2.cloned.1.call-update
  164.9 0.0 all-reduce.2.cloned.1.call-start
  165.0 70.5 %reduce-scatter.2.cloned.1.call-done = f32[128,640]{0,1:T(8,128)} async-done(((f32[2048,640]{0,1:T(8,128)}), f32[128,640]{0,1:T(8,128)}) %reduce-scatter.2.cloned.1.call-update) | async-done | bytes 327696 | tf_op jit(solution)/shard_map/reduce_scatter | solution.py:40
  235.5 2.6 fusion.35
  238.1 119.0 %all-reduce.2.cloned.1.call-done = f32[512,512]{1,0:T(8,128)} async-done(((f32[512,512]{1,0:T(8,128)}), f32[512,512]{1,0:T(8,128)}) %all-reduce.2.cloned.1.call-update) | async-done | bytes 1048592 | tf_op jit(solution)/shard_map/psum | solution.py:50
  357.1 2.7 collective-permute-start
  359.8 9.2 %copy.11 = f32[2048,1024]{1,0:T(8,128)} copy(f32[2048,1024]{0,1:T(8,128)} %copy-done.1) | data formatting | bytes 16777216
  369.1 0.8 copy.12
  369.9 0.7 copy.13
  370.6 13.1 %collective-permute-done = f32[512,512]{1,0:T(8,128)} collective-permute-done((f32[512,512]{1,0:T(8,128)}, f32[512,512]{1,0:T(8,128)}, u32[]{:S(2)}, u32[]{:S(2)}) %collective-permute-start) | collective-permute-done | bytes 1048608 | tf_op jit(solution)/shard_map/ppermute | solution.py:52
  383.7 2.4 multiply_bitcast_fusion
  (33 shorter events, 0.3 us)
Async XLA Ops:
  7.2 147.1 %copy-start = (f32[1024,512]{1,0:T(8,128)S(1)}, f32[1024,512]{1,0:T(8,128)}, u32[]{:S(2)}) copy-start(f32[1024,512]{1,0:T(8,128)} %param.11) | copy-start | bytes 6291460
  7.2 77.2 %all-gather.3.cloned.1.call-start = ((), (), s32[]{:S(2)}) async-start(), calls=%async_computation.1 | async-start | bytes 4718592 | tf_op jit(solution)/shard_map/all_gather | solution.py:19
  7.9 128.2 %all-gather.5.cloned.1.call-start = ((), (), s32[]{:S(2)}) async-start(), calls=%async_computation.2 | async-start | bytes 8912896 | tf_op jit(solution)/shard_map/all_gather | solution.py:20
  8.7 226.8 %reduce-scatter.2.cloned.1.call-start = ((), (), s32[]{:S(2)}) async-start(), calls=%async_computation.3 | async-start | bytes 5570560 | tf_op jit(solution)/shard_map/reduce_scatter | solution.py:40
  8.7 9.2 %copy-start.3 = (s32[1024]{0:T(1024)S(1)}, s32[1024]{0:T(1024)}, u32[]{:S(2)}) copy-start(s32[1024]{0:T(1024)} %param.9) | copy-start | bytes 12292
  154.0 7.9 %copy-start.1 = (f32[2048,1024]{0,1:T(8,128)}, f32[2048,1024]{0,1:T(8,128)S(1)}, u32[]{:S(2)}) copy-start(f32[2048,1024]{0,1:T(8,128)S(1)} %bitcast_subtract_fusion) | copy-start | bytes 25165828
  164.9 192.2 %all-reduce.2.cloned.1.call-start = ((), (), s32[]{:S(2)}) async-start(), calls=%async_computation.4 | async-start | bytes 2097152 | tf_op jit(solution)/shard_map/psum | solution.py:50
  238.1 131.0 %slice-start = ((f32[128,640]{0,1:T(8,128)}), f32[128,512]{0,1:T(8,128)S(1)}, s32[]{:S(2)}) async-start(f32[128,640]{0,1:T(8,128)} %reduce-scatter.2.cloned.1.call-done), calls=%async_computation.5 | async-start | bytes 524288 | tf_op jit(solution)/shard_map/slice | solution.py:41
  238.1 131.8 %slice-start.1 = ((f32[128,640]{0,1:T(8,128)}), f32[128,128]{0,1:T(8,128)S(1)}, s32[]{:S(2)}) async-start(f32[128,640]{0,1:T(8,128)} %reduce-scatter.2.cloned.1.call-done), calls=%async_computation.6 | async-start | bytes 131072 | tf_op jit(solution)/shard_map/slice | solution.py:42
  357.1 26.6 %copy-start.2 = (f32[512,512]{1,0:T(8,128)S(1)}, f32[512,512]{1,0:T(8,128)}, u32[]{:S(2)}) copy-start(f32[512,512]{1,0:T(8,128)} %all-reduce.2.cloned.1.call-done) | copy-start | bytes 3145732
  357.1 26.6 %collective-permute-start = (f32[512,512]{1,0:T(8,128)}, f32[512,512]{1,0:T(8,128)}, u32[]{:S(2)}, u32[]{:S(2)}) collective-permute-start(f32[512,512]{1,0:T(8,128)} %all-reduce.2.cloned.1.call-done), channel_id=1, source_target_pairs={{0,16},{16,0},{32,48},{48,32},{64,80},{80,64},{96,112},{112,96},{1... | collective-permute-start | bytes 3145736 | tf_op jit(solution)/shard_map/ppermute | solution.py:52
Sparse Core Ops, SparseCore 0:
  10.3 74.0 all-gather.2
  86.1 49.9 all-gather.4
  165.0 70.3 reduce-scatter.1
  238.4 118.7 all-reduce.1
where the time goes:
time: 393 us
  waiting for transfers between devices  296 us (75%)
  matrix products  45.9 us (12%)
  local copies, waits for them, and re-layouts  28.6 us (7%)
  between operations  14 us (4%)
  other arithmetic  5.64 us (1%)
    psum x1, waiting for transfers between devices, body(): gram = lax.psum(gram, 'col')  119 us
    reduce_scatter x1, waiting for transfers between devices, body(): own = lax.psum_scatter(both, 'col', scatter_dimension=0, tiled=True)  70.5 us
    all_gather x1, waiting for transfers between devices, body(): upper_full = lax.all_gather(panel_rows, 'row', axis=0, tiled=True)  66.5 us
    dot_general x3, matrix products, product(): jnp.dot(left, right, precision=lax.Precision.HIGH, preferred_element_type...  43.3 us
    all_gather x1, waiting for transfers between devices, body(): left = lax.all_gather(panel_columns, 'col', axis=1, tiled=True)  25.2 us
    unnamed x12, local copies, waits for them, and re-layouts  20 us
    ppermute x1, waiting for transfers between devices, body(): gram = gram + lax.ppermute(gram, 'row', route)  13.1 us
    gather x1, local copies, waits for them, and re-layouts, body(): upper = jnp.take(upper_full, pivots, axis=0)  8.63 us
  transfers between devices with their start and end apart: 5, of which 5 were waited for; matrix products, arithmetic and copies ran while one was open for 12% of the time, Pallas kernels for 0%

commit v1 on v0

--- a/solution.py
+++ b/solution.py
@@ -47,7 +47,7 @@
         precision=lax.Precision.HIGH,
         preferred_element_type=jnp.float32,
     )
-    gram = lax.psum(gram, "col")
+    gram = lax.all_gather(gram, axis_name="col").sum(axis=0)
     route = [(i, i ^ 1) for i in range(row_count)]
     gram = gram + lax.ppermute(gram, "row", route)
     group_gram = (gram / (2 * height))[None]

time: 393 us -> 373 us (0.949)
  waiting for transfers between devices: 296 us -> 267 us
  other arithmetic: 5.64 us -> 13.6 us
    psum x1 -> x0, waiting for transfers between devices: 119 us -> none  [body(): gram = lax.psum(gram, 'col')]
    all_gather x0 -> x1, waiting for transfers between devices: none -> 90.1 us  [body(): gram = lax.all_gather(gram, axis_name='col').sum(axis=0)]
    reduce_sum x0 -> x1, other arithmetic: none -> 7.91 us  [body(): gram = lax.all_gather(gram, axis_name='col').sum(axis=0)]
    unnamed x12 -> x10, local copies, waits for them, and re-layouts: 20 us -> 20 us
where the time goes in v1:
time: 373 us; the launch traced here: 372 us
  waiting for transfers between devices  267 us (72%)
  matrix products  45.9 us (12%)
  local copies, waits for them, and re-layouts  28.6 us (8%)
  between operations  14 us (4%)
  other arithmetic  13.6 us (4%)
    all_gather x1, waiting for transfers between devices, body(): gram = lax.all_gather(gram, axis_name='col').sum(axis=0)  90.1 us
    reduce_scatter x1, waiting for transfers between devices, body(): own = lax.psum_scatter(both, 'col', scatter_dimension=0, tiled=True)  70.5 us
    all_gather x1, waiting for transfers between devices, body(): upper_full = lax.all_gather(panel_rows, 'row', axis=0, tiled=True)  66.5 us
    dot_general x3, matrix products, product(): jnp.dot(left, right, precision=lax.Precision.HIGH, preferred_element_type...  43.3 us
    all_gather x1, waiting for transfers between devices, body(): left = lax.all_gather(panel_columns, 'col', axis=1, tiled=True)  25.2 us
    unnamed x10, local copies, waits for them, and re-layouts  20 us
    ppermute x1, waiting for transfers between devices, body(): gram = gram + lax.ppermute(gram, 'row', route)  13.1 us
    gather x1, local copies, waits for them, and re-layouts, body(): upper = jnp.take(upper_full, pivots, axis=0)  8.59 us
  transfers between devices with their start and end apart: 5, of which 5 were waited for; matrix products, arithmetic and copies ran while one was open for 12% of the time, Pallas kernels for 0%

profile of v1, /device:TPU:0, one launch (start us, length us, event | category | flops | bytes accessed | tf_op | source)
XLA Modules:
  0.0 372.1 jit_solution(11364131797273274324)
XLA Ops:
  7.2 0.0 all-gather.5.cloned.1.call-start
  7.2 0.7 all-gather.5.cloned.1.call-update
  7.9 0.0 all-gather.7.cloned.1.call-start
  8.0 0.7 all-gather.7.cloned.1.call-update
  8.7 0.0 reduce-scatter.2.cloned.1.call-start
  8.7 9.1 %copy.10 = f32[2048,1024]{0,1:T(8,128)} copy(f32[2048,1024]{1,0:T(8,128)} %param.6) | data formatting | bytes 16777216 | tf_op args[0]
  17.9 66.5 %all-gather.5.cloned.1.call-done = f32[1024,1024]{1,0:T(8,128)} async-done(((f32[128,1024]{1,0:T(8,128)}), f32[1024,1024]{1,0:T(8,128)}) %all-gather.5.cloned.1.call-update) | async-done | bytes 4194320 | tf_op jit(solution)/shard_map/all_gather | solution.py:19
  84.4 8.6 %gather_fusion = f32[1024,1024]{1,0:T(8,128)} fusion(f32[1024,1024]{1,0:T(8,128)} %all-gather.5.cloned.1.call-done, s32[1024]{0:T(1024)S(1)} %fusion.32), kind=kCustom, calls=%fused_computation | custom fusion | bytes 8392704 | tf_op jit(solution)/shard_map/jit(_take)/gather | solution.py:21
  93.0 17.9 %fusion.5 = f32[1024,1024]{1,0:T(8,128)} fusion(f32[1024,1024]{1,0:T(8,128)} %param.10, f32[1024,1024]{1,0:T(8,128)} %gather_fusion, pred[1024]{0:T(1024)(128)(4,1)S(1)} %compare_and_fusion), kind=kOutput, calls=%fused_computation.8 | convolution fusion | flops 6443499520 | bytes 12583936 | tf_op jit(solution)/shard_map/dot_general | solution.py:10
  110.9 25.2 %all-gather.7.cloned.1.call-done = f32[2048,1024]{0,1:T(8,128)} async-done(((f32[2048,64]{0,1:T(8,128)}), f32[2048,1024]{0,1:T(8,128)}) %all-gather.7.cloned.1.call-update) | async-done | bytes 8388624 | tf_op jit(solution)/shard_map/all_gather | solution.py:20
  136.1 17.8 %bitcast_subtract_fusion = f32[2048,1024]{0,1:T(8,128)S(1)} fusion(f32[2048,1024]{0,1:T(8,128)} %copy.10, f32[1024,1024]{1,0:T(8,128)} %fusion.5, f32[2048,1024]{0,1:T(8,128)} %all-gather.7.cloned.1.call-done), kind=kOutput, calls=%fused_computation.1 | convolution fusion | flops 12886999040 | bytes 29360128 | tf_op jit(solution)/shard_map/dot_general | solution.py:10
  154.3 7.6 %fusion = f32[2048,512]{0,1:T(8,128)S(1)} fusion(f32[1024,512]{1,0:T(8,128)S(1)} %copy-done, f32[2048,1024]{0,1:T(8,128)S(1)} %bitcast_subtract_fusion, s32[2048]{0:T(1024)S(1)} %add_select_fusion, s32[1024]{0:T(1024)S(1)} %add_select_fusion.1), kind=kOutput, calls=%fused_computation.2 | convolution fusion | flops 6446645248 | bytes 14692352 | tf_op jit(solution)/shard_map/dot_general | solution.py:10
  161.9 3.0 pad_maximum_fusion
  164.9 0.0 all-gather.9.cloned.1.call-start
  165.0 70.5 %reduce-scatter.2.cloned.1.call-done = f32[128,640]{0,1:T(8,128)} async-done(((f32[2048,640]{0,1:T(8,128)}), f32[128,640]{0,1:T(8,128)}) %reduce-scatter.2.cloned.1.call-update) | async-done | bytes 327696 | tf_op jit(solution)/shard_map/reduce_scatter | solution.py:40
  235.5 2.6 fusion.35
  238.1 90.1 %all-gather.9.cloned.1.call-done = f32[8192,512]{1,0:T(8,128)} async-done(((f32[512,512]{1,0:T(8,128)}), f32[8192,512]{1,0:T(8,128)}) %all-gather.9.cloned.1.call-update) | async-done | bytes 16777232 | tf_op jit(solution)/shard_map/all_gather | solution.py:50
  328.2 7.9 %reduce_sum.9 = f32[512,512]{1,0:T(8,128)S(1)} reduce(f32[16,512,512]{2,1,0:T(8,128)} %bitcast.9, f32[]{:T(128)} %constant.59.clone.1), dimensions={0}, to_apply=%region_1.2 | reduce | flops 3932160 | bytes 17825796 | tf_op jit(solution)/shard_map/reduce_sum | solution.py:50
  336.1 3.1 collective-permute-start
  339.2 9.2 %copy.11 = f32[2048,1024]{1,0:T(8,128)} copy(f32[2048,1024]{0,1:T(8,128)} %copy-done.1) | data formatting | bytes 16777216
  348.5 0.7 copy.13
  349.2 0.8 copy.12
  350.0 13.1 %collective-permute-done = f32[512,512]{1,0:T(8,128)} collective-permute-done((f32[512,512]{1,0:T(8,128)S(1)}, f32[512,512]{1,0:T(8,128)}, u32[]{:S(2)}, u32[]{:S(2)}) %collective-permute-start) | collective-permute-done | bytes 1048608 | tf_op jit(solution)/shard_map/ppermute | solution.py:52
  363.1 2.4 multiply_bitcast_fusion
  (32 shorter events, 0.3 us)
Async XLA Ops:
  7.2 147.1 %copy-start = (f32[1024,512]{1,0:T(8,128)S(1)}, f32[1024,512]{1,0:T(8,128)}, u32[]{:S(2)}) copy-start(f32[1024,512]{1,0:T(8,128)} %param.11) | copy-start | bytes 6291460
  7.2 77.2 %all-gather.5.cloned.1.call-start = ((), (), s32[]{:S(2)}) async-start(), calls=%async_computation.1 | async-start | bytes 4718592 | tf_op jit(solution)/shard_map/all_gather | solution.py:19
  7.9 128.2 %all-gather.7.cloned.1.call-start = ((), (), s32[]{:S(2)}) async-start(), calls=%async_computation.2 | async-start | bytes 8912896 | tf_op jit(solution)/shard_map/all_gather | solution.py:20
  8.7 226.8 %reduce-scatter.2.cloned.1.call-start = ((), (), s32[]{:S(2)}) async-start(), calls=%async_computation.3 | async-start | bytes 5570560 | tf_op jit(solution)/shard_map/reduce_scatter | solution.py:40
  8.7 9.2 %copy-start.2 = (s32[1024]{0:T(1024)S(1)}, s32[1024]{0:T(1024)}, u32[]{:S(2)}) copy-start(s32[1024]{0:T(1024)} %param.9) | copy-start | bytes 12292
  154.0 7.9 %copy-start.1 = (f32[2048,1024]{0,1:T(8,128)}, f32[2048,1024]{0,1:T(8,128)S(1)}, u32[]{:S(2)}) copy-start(f32[2048,1024]{0,1:T(8,128)S(1)} %bitcast_subtract_fusion) | copy-start | bytes 25165828
  164.9 163.3 %all-gather.9.cloned.1.call-start = ((), (), s32[]{:S(2)}) async-start(), calls=%async_computation.4 | async-start | bytes 17825792 | tf_op jit(solution)/shard_map/all_gather | solution.py:50
  336.1 12.4 %slice-start = ((f32[128,640]{0,1:T(8,128)}), f32[128,128]{0,1:T(8,128)S(1)}, s32[]{:S(2)}) async-start(f32[128,640]{0,1:T(8,128)} %reduce-scatter.2.cloned.1.call-done), calls=%async_computation.5 | async-start | bytes 131072 | tf_op jit(solution)/shard_map/slice | solution.py:42
  336.1 13.1 %slice-start.1 = ((f32[128,640]{0,1:T(8,128)}), f32[128,512]{0,1:T(8,128)S(1)}, s32[]{:S(2)}) async-start(f32[128,640]{0,1:T(8,128)} %reduce-scatter.2.cloned.1.call-done), calls=%async_computation.6 | async-start | bytes 524288 | tf_op jit(solution)/shard_map/slice | solution.py:41
  336.1 27.0 %collective-permute-start = (f32[512,512]{1,0:T(8,128)S(1)}, f32[512,512]{1,0:T(8,128)}, u32[]{:S(2)}, u32[]{:S(2)}) collective-permute-start(f32[512,512]{1,0:T(8,128)S(1)} %reduce_sum.9), channel_id=1, source_target_pairs={{0,16},{16,0},{32,48},{48,32},{64,80},{80,64},{96,112},{112,96},{1... | collective-permute-start | bytes 3145736 | tf_op jit(solution)/shard_map/ppermute | solution.py:52
Sparse Core Ops, SparseCore 0:
  10.3 74.0 all-gather.4
  86.1 49.9 all-gather.6
  165.0 70.3 reduce-scatter.1
  238.2 89.9 all-gather.8
